TPU v7x, 32 devices: a whole 2x2x4 slice. The times are simulated.
32 devices in a mesh: dp: 2 (over core), ctx: 4 (over z), tensor: 4 (over y, x).
Axes of the slice: x: 2, y: 2, z: 4, core: 2. Of those that a mesh axis runs over, the one named last changes fastest.
Arguments:
- tokens: bfloat16 [4096, 2048], P(('dp', 'ctx')), may hold values from -6 to 6
- lengths: int32 [2, 13], P('dp'), may hold values from 1 to 819, 2048 in all within a row
- parents: int32 [2, 13], P('dp'), may hold values from 0 to 4, as said below
- w_query: bfloat16 [2048, 2048], P(('dp', 'ctx'), 'tensor'), may hold values from -0.125 to 0.125
- w_key: bfloat16 [2048, 1024], P(('dp', 'ctx'), 'tensor'), may hold values from -0.125 to 0.125
- w_value: bfloat16 [2048, 1024], P(('dp', 'ctx'), 'tensor'), may hold values from -0.125 to 0.125
- w_out: bfloat16 [2048, 2048], P('tensor', ('dp', 'ctx')), may hold values from -1.5 to 1.5
- w_gate: bfloat16 [2048, 6144], P(('dp', 'ctx'), 'tensor'), may hold values from -0.125 to 0.125
- w_up: bfloat16 [2048, 6144], P(('dp', 'ctx'), 'tensor'), may hold values from -0.125 to 0.125
- w_down: bfloat16 [6144, 2048], P('tensor', ('dp', 'ctx')), may hold values from -0.078125 to 0.078125
- gain_attn: bfloat16 [2048], P(('dp', 'ctx')), may hold values from 0.099609375 to 1.8984375
- gain_mlp: bfloat16 [2048], P(('dp', 'ctx')), may hold values from 0.099609375 to 1.8984375
- gain_query: bfloat16 [128], P(('dp', 'ctx')), may hold values from 0.099609375 to 1.8984375
- gain_key: bfloat16 [128], P(('dp', 'ctx')), may hold values from 0.099609375 to 1.8984375
- cotangent: bfloat16 [4096, 2048], P(('dp', 'ctx')), may hold values from -6 to 6
Outputs:
- result: bfloat16 [4096, 2048], P(('dp', 'ctx'))
- grad_tokens: float32 [4096, 2048], P(('dp', 'ctx'))
- grad_query: float32 [2048, 2048], P(('dp', 'ctx'), 'tensor')
- grad_key: float32 [2048, 1024], P(('dp', 'ctx'), 'tensor')
- grad_value: float32 [2048, 1024], P(('dp', 'ctx'), 'tensor')
- grad_out: float32 [2048, 2048], P('tensor', ('dp', 'ctx'))
- grad_gate: float32 [2048, 6144], P(('dp', 'ctx'), 'tensor')
- grad_up: float32 [2048, 6144], P(('dp', 'ctx'), 'tensor')
- grad_down: float32 [6144, 2048], P('tensor', ('dp', 'ctx'))
- grad_gain_attn: float32 [2048], P(('dp', 'ctx'))
- grad_gain_mlp: float32 [2048], P(('dp', 'ctx'))
- grad_gain_query: float32 [128], P(('dp', 'ctx'))
- grad_gain_key: float32 [128], P(('dp', 'ctx'))
Inputs may be any that keep to these rules, and one draw needn't show every extreme that they name: lengths[t, s] counts the tokens of segment s of tree t; the segments lie in order and each tree's lengths sum to 2048. parents[t, s] is the segment from which segment s of tree t hangs; segments 0 to 4 name 0 (segment 0 is the root), segments 5 to 12 name one of 1 to 4.
All inputs are finite; a program needn't handle non-finite values.
Results may differ from a plain program's by a relative error of at most 0.02.
Values may be sent and summed in bfloat16 or wider, within the bound.
No kernel may reach another device: no remote copies, remote signals or barrier semaphores. Data moves between devices by JAX's collectives and lax.ppermute only.
A program may use at most 192 MiB of HBM per device.

v0:
```python
import math
import jax
import jax.numpy as jnp
from jax import lax
from jax.sharding import PartitionSpec as P

HEAD_DIM = 128
EPS = 1e-06
THETA = 1000000.0
PRECISE = lax.Precision.HIGHEST


def norm_rows(values, gain_vec):
    scales = lax.rsqrt(jnp.mean(values * values, axis=-1, keepdims=True) + EPS)
    return (values * scales * gain_vec, scales)


def norm_back(grad_in, values, gain_vec, scales):
    upstream = grad_in * gain_vec
    inner_mean = jnp.mean(upstream * values, axis=-1, keepdims=True)
    return (
        scales * upstream - values * scales * scales * scales * inner_mean,
        grad_in * values * scales,
    )


def rotate_pairs(values, cosine, sine_vals):
    half_dim = values.shape[-1] // 2
    first_half = values[..., :half_dim]
    second_half = values[..., half_dim:]
    return jnp.concatenate(
        [
            first_half * cosine - second_half * sine_vals,
            second_half * cosine + first_half * sine_vals,
        ],
        axis=-1,
    )


def rotate_back(values, cosine, sine_vals):
    half_dim = values.shape[-1] // 2
    first_half = values[..., :half_dim]
    second_half = values[..., half_dim:]
    return jnp.concatenate(
        [
            first_half * cosine + second_half * sine_vals,
            second_half * cosine - first_half * sine_vals,
        ],
        axis=-1,
    )


def inner_rows(left, right):
    return lax.dot_general(
        left, right, (((0,), (0,)), ((), ())), preferred_element_type=jnp.float32
    )


def outer_cols(left, right):
    return lax.dot_general(
        left, right, (((1,), (1,)), ((), ())), preferred_element_type=jnp.float32
    )


def tensor_sum(values):
    return lax.psum(values, "tensor")


def tree_layout(lengths, parents, tree_total):
    seg_count = lengths.shape[0]
    index = jnp.arange(seg_count, dtype=jnp.int32)
    direct = ((parents[:, None] == index[None, :]) & (parents[:, None] != index[:, None])).astype(
        jnp.float32
    )
    reach = direct
    for closure_step in range(4):
        reach = jnp.minimum(reach + jnp.dot(reach, reach, precision=PRECISE), 1.0)
    ends = jnp.cumsum(lengths, dtype=jnp.int32)
    starts = ends - lengths
    offset = jnp.dot(reach, lengths.astype(jnp.float32), precision=PRECISE)
    places = jnp.arange(tree_total, dtype=jnp.int32)
    member = (starts[None, :] <= places[:, None]).astype(jnp.int32)
    segment_ids = jnp.sum(member, axis=1, dtype=jnp.int32) - 1
    onehot = (segment_ids[:, None] == index[None, :]).astype(jnp.float32)
    base = jnp.dot(onehot, offset - starts.astype(jnp.float32), precision=PRECISE)
    position = places.astype(jnp.float32) + base
    return (segment_ids, onehot, reach, position)


def on_device(
    tokens,
    lengths,
    parents,
    w_query,
    w_key,
    w_value,
    w_out,
    w_gate,
    w_up,
    w_down,
    gain_attn,
    gain_mlp,
    gain_query,
    gain_key,
    cotangent,
):
    row_count = tokens.shape[0]
    tree_total = row_count * lax.axis_size("ctx")
    start_row = lax.axis_index("ctx") * row_count
    attn_set = (
        lax.all_gather(w_query, ("dp", "ctx"), axis=0, tiled=True),
        lax.all_gather(w_key, ("dp", "ctx"), axis=0, tiled=True),
        lax.all_gather(w_value, ("dp", "ctx"), axis=0, tiled=True),
        lax.all_gather(w_out, ("dp", "ctx"), axis=1, tiled=True),
        lax.all_gather(gain_attn, ("dp", "ctx"), axis=0, tiled=True),
        lax.all_gather(gain_query, ("dp", "ctx"), axis=0, tiled=True),
        lax.all_gather(gain_key, ("dp", "ctx"), axis=0, tiled=True),
    )
    mlp_set = (
        lax.all_gather(w_gate, ("dp", "ctx"), axis=0, tiled=True),
        lax.all_gather(w_up, ("dp", "ctx"), axis=0, tiled=True),
        lax.all_gather(w_down, ("dp", "ctx"), axis=1, tiled=True),
        lax.all_gather(gain_mlp, ("dp", "ctx"), axis=0, tiled=True),
    )
    wq_full, wk_full, wv_full, wo_full, gain_one, gain_q, gain_k = attn_set
    wg_full, wu_full, wd_full, gain_two = mlp_set
    segment_all, onehot_all, reach, position_all = tree_layout(lengths[0], parents[0], tree_total)
    segment_here = lax.dynamic_slice_in_dim(segment_all, start_row, row_count)
    onehot_here = lax.dynamic_slice_in_dim(onehot_all, start_row, row_count)
    position = lax.dynamic_slice_in_dim(position_all, start_row, row_count)
    place_here = start_row + jnp.arange(row_count, dtype=jnp.int32)
    place_all = jnp.arange(tree_total, dtype=jnp.int32)
    ancestor = (
        jnp.dot(jnp.dot(onehot_here, reach, precision=PRECISE), onehot_all.T, precision=PRECISE)
        > 0.5
    )
    allowed = (segment_here[:, None] == segment_all[None, :]) & (
        place_all[None, :] <= place_here[:, None]
    ) | ancestor
    half_dim = HEAD_DIM // 2
    frequency = jnp.exp(
        jnp.arange(half_dim, dtype=jnp.float32) * (-2.0 * math.log(THETA) / HEAD_DIM)
    )
    angles = position[:, None] * frequency[None, :]
    cosine = jnp.cos(angles)[:, None, :]
    sine_vals = jnp.sin(angles)[:, None, :]
    score_scale = 1.0 / math.sqrt(HEAD_DIM)
    inputs = tokens.astype(jnp.float32)
    gain_onef = gain_one.astype(jnp.float32)
    normed_f, scale_one = norm_rows(inputs, gain_onef)
    normed_attn = normed_f.astype(jnp.bfloat16)
    q_raw = jnp.dot(normed_attn, wq_full, preferred_element_type=jnp.float32)
    k_raw = jnp.dot(normed_attn, wk_full, preferred_element_type=jnp.float32)
    v_bf = jnp.dot(normed_attn, wv_full, preferred_element_type=jnp.float32).astype(jnp.bfloat16)
    heads_here = q_raw.shape[1] // HEAD_DIM
    kv_here = k_raw.shape[1] // HEAD_DIM
    group_size = heads_here // kv_here
    gain_qf = gain_q.astype(jnp.float32)
    gain_kf = gain_k.astype(jnp.float32)
    q_heads = q_raw.reshape(row_count, heads_here, HEAD_DIM)
    k_heads = k_raw.reshape(row_count, kv_here, HEAD_DIM)
    q_normed, q_scales = norm_rows(q_heads, gain_qf)
    k_normed, k_scales = norm_rows(k_heads, gain_kf)
    q_bf = rotate_pairs(q_normed, cosine, sine_vals).astype(jnp.bfloat16)
    k_bf = rotate_pairs(k_normed, cosine, sine_vals).astype(jnp.bfloat16)
    k_all, v_all = (
        lax.all_gather(k_bf.reshape(row_count, kv_here * HEAD_DIM), "ctx", axis=0, tiled=True),
        lax.all_gather(v_bf, "ctx", axis=0, tiled=True),
    )
    k_all = k_all.reshape(tree_total, kv_here, HEAD_DIM)
    v_all = v_all.reshape(tree_total, kv_here, HEAD_DIM)
    q_grouped = q_bf.reshape(row_count, kv_here, group_size, HEAD_DIM)
    scores = (
        jnp.einsum("tkgd,skd->kgts", q_grouped, k_all, preferred_element_type=jnp.float32)
        * score_scale
    )
    scores = jnp.where(allowed[None, None], scores, -1e30)
    row_max = jnp.max(scores, axis=-1, keepdims=True)
    weights = jnp.exp(scores - row_max)
    prob_all = weights / jnp.sum(weights, axis=-1, keepdims=True)
    prob_bf = prob_all.astype(jnp.bfloat16)
    mixture = jnp.einsum("kgts,skd->tkgd", prob_bf, v_all, preferred_element_type=jnp.float32)
    mixture_bf = mixture.reshape(row_count, heads_here * HEAD_DIM).astype(jnp.bfloat16)
    attn_term = jnp.dot(mixture_bf, wo_full, preferred_element_type=jnp.float32)
    gain_twof = gain_two.astype(jnp.float32)
    hidden = inputs + tensor_sum(attn_term)
    normed_g, scale_two = norm_rows(hidden, gain_twof)
    normed_mlp = normed_g.astype(jnp.bfloat16)
    gate_pre = jnp.dot(normed_mlp, wg_full, preferred_element_type=jnp.float32)
    up_pre = jnp.dot(normed_mlp, wu_full, preferred_element_type=jnp.float32)
    gate_sig = jax.nn.sigmoid(gate_pre)
    gate_act = gate_pre * gate_sig
    inner_bf = (gate_act * up_pre).astype(jnp.bfloat16)
    mlp_term = jnp.dot(inner_bf, wd_full, preferred_element_type=jnp.float32)
    result = (hidden + tensor_sum(mlp_term)).astype(jnp.bfloat16)
    grad_result = cotangent.astype(jnp.float32)
    grad_down = inner_rows(inner_bf, cotangent)
    grad_inner = outer_cols(cotangent, wd_full)
    grad_gate_pre = (grad_inner * up_pre * gate_sig * (1.0 + gate_pre * (1.0 - gate_sig))).astype(
        jnp.bfloat16
    )
    grad_up_pre = (grad_inner * gate_act).astype(jnp.bfloat16)
    grad_gate = inner_rows(normed_mlp, grad_gate_pre)
    grad_up = inner_rows(normed_mlp, grad_up_pre)
    mlp_back_term = outer_cols(grad_gate_pre, wg_full) + outer_cols(grad_up_pre, wu_full)
    grad_normed_mlp = tensor_sum(mlp_back_term)
    grad_hidden_norm, gain_two_terms = norm_back(grad_normed_mlp, hidden, gain_twof, scale_two)
    grad_gain_mlp = jnp.sum(gain_two_terms, axis=0)
    grad_hidden = grad_result + grad_hidden_norm
    grad_attn_bf = grad_hidden.astype(jnp.bfloat16)
    grad_out = inner_rows(mixture_bf, grad_attn_bf)
    grad_mixture = (
        outer_cols(grad_attn_bf, wo_full)
        .astype(jnp.bfloat16)
        .reshape(row_count, kv_here, group_size, HEAD_DIM)
    )
    grad_probs = jnp.einsum(
        "tkgd,skd->kgts", grad_mixture, v_all, preferred_element_type=jnp.float32
    )
    grad_v_all = jnp.einsum(
        "kgts,tkgd->skd", prob_bf, grad_mixture, preferred_element_type=jnp.float32
    )
    row_total = jnp.sum(prob_all * grad_probs, axis=-1, keepdims=True)
    grad_scores = (prob_all * (grad_probs - row_total)).astype(jnp.bfloat16)
    grad_q = (
        jnp.einsum("kgts,skd->tkgd", grad_scores, k_all, preferred_element_type=jnp.float32)
        * score_scale
    )
    grad_k_all = (
        jnp.einsum("kgts,tkgd->skd", grad_scores, q_grouped, preferred_element_type=jnp.float32)
        * score_scale
    )
    grad_k, grad_v = (
        lax.psum_scatter(
            grad_k_all.reshape(tree_total, kv_here * HEAD_DIM),
            "ctx",
            scatter_dimension=0,
            tiled=True,
        ),
        lax.psum_scatter(
            grad_v_all.reshape(tree_total, kv_here * HEAD_DIM),
            "ctx",
            scatter_dimension=0,
            tiled=True,
        ),
    )
    grad_q = (
        grad_q.reshape(row_count, heads_here, HEAD_DIM).astype(jnp.bfloat16).astype(jnp.float32)
    )
    grad_k = grad_k.reshape(row_count, kv_here, HEAD_DIM).astype(jnp.bfloat16).astype(jnp.float32)
    grad_v_bf = grad_v.astype(jnp.bfloat16)
    grad_q_heads, q_gain_terms = norm_back(
        rotate_back(grad_q, cosine, sine_vals), q_heads, gain_qf, q_scales
    )
    grad_k_heads, k_gain_terms = norm_back(
        rotate_back(grad_k, cosine, sine_vals), k_heads, gain_kf, k_scales
    )
    grad_q_raw = grad_q_heads.reshape(row_count, heads_here * HEAD_DIM).astype(jnp.bfloat16)
    grad_k_raw = grad_k_heads.reshape(row_count, kv_here * HEAD_DIM).astype(jnp.bfloat16)
    grad_query = inner_rows(normed_attn, grad_q_raw)
    grad_key = inner_rows(normed_attn, grad_k_raw)
    grad_value = inner_rows(normed_attn, grad_v_bf)
    partial_value = (
        outer_cols(grad_q_raw, wq_full)
        + outer_cols(grad_k_raw, wk_full)
        + outer_cols(grad_v_bf, wv_full)
    )
    q_gain_part = jnp.sum(q_gain_terms, axis=(0, 1))
    k_gain_part = jnp.sum(k_gain_terms, axis=(0, 1))
    grad_normed_attn, grad_gain_query, grad_gain_key = (
        lax.psum(partial_value.astype(jnp.bfloat16), "tensor").astype(jnp.float32),
        lax.psum(q_gain_part.astype(jnp.bfloat16), "tensor").astype(jnp.float32),
        lax.psum(k_gain_part.astype(jnp.bfloat16), "tensor").astype(jnp.float32),
    )
    grad_input_norm, gain_one_terms = norm_back(grad_normed_attn, inputs, gain_onef, scale_one)
    grad_tokens = grad_hidden + grad_input_norm
    grad_gain_attn = jnp.sum(gain_one_terms, axis=0)
    (
        grad_query,
        grad_key,
        grad_value,
        grad_out,
        grad_gate,
        grad_up,
        grad_down,
        grad_gain_attn,
        grad_gain_mlp,
        grad_gain_query,
        grad_gain_key,
    ) = (
        lax.psum_scatter(
            grad_query.astype(jnp.bfloat16), ("dp", "ctx"), scatter_dimension=0, tiled=True
        ).astype(jnp.float32),
        lax.psum_scatter(
            grad_key.astype(jnp.bfloat16), ("dp", "ctx"), scatter_dimension=0, tiled=True
        ).astype(jnp.float32),
        lax.psum_scatter(
            grad_value.astype(jnp.bfloat16), ("dp", "ctx"), scatter_dimension=0, tiled=True
        ).astype(jnp.float32),
        lax.psum_scatter(
            grad_out.astype(jnp.bfloat16), ("dp", "ctx"), scatter_dimension=1, tiled=True
        ).astype(jnp.float32),
        lax.psum_scatter(
            grad_gate.astype(jnp.bfloat16), ("dp", "ctx"), scatter_dimension=0, tiled=True
        ).astype(jnp.float32),
        lax.psum_scatter(
            grad_up.astype(jnp.bfloat16), ("dp", "ctx"), scatter_dimension=0, tiled=True
        ).astype(jnp.float32),
        lax.psum_scatter(
            grad_down.astype(jnp.bfloat16), ("dp", "ctx"), scatter_dimension=1, tiled=True
        ).astype(jnp.float32),
        lax.psum_scatter(
            grad_gain_attn.astype(jnp.bfloat16), ("dp", "ctx"), scatter_dimension=0, tiled=True
        ).astype(jnp.float32),
        lax.psum_scatter(
            grad_gain_mlp.astype(jnp.bfloat16), ("dp", "ctx"), scatter_dimension=0, tiled=True
        ).astype(jnp.float32),
        lax.psum_scatter(
            grad_gain_query.astype(jnp.bfloat16), ("dp", "ctx"), scatter_dimension=0, tiled=True
        ).astype(jnp.float32),
        lax.psum_scatter(
            grad_gain_key.astype(jnp.bfloat16), ("dp", "ctx"), scatter_dimension=0, tiled=True
        ).astype(jnp.float32),
    )
    return (
        result,
        grad_tokens,
        grad_query,
        grad_key,
        grad_value,
        grad_out,
        grad_gate,
        grad_up,
        grad_down,
        grad_gain_attn,
        grad_gain_mlp,
        grad_gain_query,
        grad_gain_key,
    )


def solution(mesh):
    placed = (
        P(("dp", "ctx"), None),
        P("dp", None),
        P("dp", None),
        P(("dp", "ctx"), "tensor"),
        P(("dp", "ctx"), "tensor"),
        P(("dp", "ctx"), "tensor"),
        P("tensor", ("dp", "ctx")),
        P(("dp", "ctx"), "tensor"),
        P(("dp", "ctx"), "tensor"),
        P("tensor", ("dp", "ctx")),
        P(("dp", "ctx")),
        P(("dp", "ctx")),
        P(("dp", "ctx")),
        P(("dp", "ctx")),
        P(("dp", "ctx"), None),
    )
    return jax.shard_map(
        on_device,
        mesh=mesh,
        in_specs=placed,
        out_specs=(
            P(("dp", "ctx"), None),
            P(("dp", "ctx"), None),
            P(("dp", "ctx"), "tensor"),
            P(("dp", "ctx"), "tensor"),
            P(("dp", "ctx"), "tensor"),
            P("tensor", ("dp", "ctx")),
            P(("dp", "ctx"), "tensor"),
            P(("dp", "ctx"), "tensor"),
            P("tensor", ("dp", "ctx")),
            P(("dp", "ctx")),
            P(("dp", "ctx")),
            P(("dp", "ctx")),
            P(("dp", "ctx")),
        ),
        check_vma=False,
    )
```

profile of v0, /device:TPU:0, one launch (start us, length us, event | category | flops | bytes accessed | tf_op | source)
XLA Modules:
  0.0 1460.9 jit_solution(8026323037325675424)
XLA Ops:
  9.4 17.9 %all-gather = bf16[8,1,256]{2,1,0:T(2,128)(2,1)S(1)} all-gather(bf16[1,1,256]{2,1,0:T(2,128)(2,1)S(1)} %reshape.243), channel_id=1, replica_groups=mesh['dp'=2,'ctx'=4,'tensor'=4] {'dp','ctx'}, dimensions={0}, use_global_device_ids=true | all-gather | bytes 4608 | tf_op jit(solution)/shard_map/all_gather | solution.py:115
  29.6 4.9 all-gather.12.cloned.1.call-done
  34.6 3.3 convolution_convert_fusion.8
  40.3 16.3 %all-reduce.8 = (bf16[128]{0:T(256)(128)(2,1)S(1)}, bf16[128]{0:T(256)(128)(2,1)S(1)}) all-reduce(bf16[128]{0:T(256)(128)(2,1)S(1)} %dynamic-update-slice, bf16[128]{0:T(256)(128)(2,1)S(1)} %dynamic-update-slice.1), channel_id=1, replica_groups=mesh['dp'=2,'ctx'=4,'tensor'=4] {'dp','ctx'}, use_global_device_ids=true, to_apply=%add | all-reduce | flops 256 | bytes 1024
  64.4 3.2 fusion.25
  70.3 17.6 %all-gather.14.cloned.1.call-done = bf16[2048,256]{1,0:T(8,128)(2,1)} async-done(((bf16[512,256]{1,0:T(8,128)(2,1)}), bf16[2048,256]{1,0:T(8,128)(2,1)}) %all-gather.14.cloned.1.call-update) | async-done | bytes 1048592 | tf_op jit(solution)/shard_map/all_gather | solution.py:168
  90.2 27.7 %all-gather.20.cloned.1.call-done = bf16[2048,512]{1,0:T(8,128)(2,1)} async-done(((bf16[256,512]{1,0:T(8,128)(2,1)}), bf16[2048,512]{1,0:T(8,128)(2,1)}) %all-gather.20.cloned.1.call-update) | async-done | bytes 2097168 | tf_op jit(solution)/shard_map/all_gather | solution.py:111
  122.8 24.4 %all-gather.18.cloned.1.call-done = bf16[2048,256]{0,1:T(8,128)(2,1)} async-done(((bf16[512,256]{0,1:T(8,128)(2,1)}), bf16[2048,256]{0,1:T(8,128)(2,1)}) %all-gather.18.cloned.1.call-update) | async-done | bytes 1048592 | tf_op jit(solution)/shard_map/all_gather | solution.py:167
  147.3 13.9 fusion.81
  161.2 7.6 fusion.32
  168.8 9.9 all-gather.22.cloned.1.call-done
  178.7 4.9 fusion.82
  185.8 16.4 %all-gather.1 = bf16[8,1,256]{2,1,0:T(2,128)(2,1)S(1)} all-gather(bf16[1,1,256]{2,1,0:T(2,128)(2,1)S(1)} %reshape.245), channel_id=1, replica_groups=mesh['dp'=2,'ctx'=4,'tensor'=4] {'dp','ctx'}, dimensions={0}, use_global_device_ids=true | all-gather | bytes 4608 | tf_op jit(solution)/shard_map/all_gather | solution.py:123
  202.2 84.2 %all-reduce.14.cloned.1.call-done = f32[512,2048]{1,0:T(8,128)} async-done(((f32[512,2048]{1,0:T(8,128)}), f32[512,2048]{1,0:T(8,128)}) %all-reduce.14.cloned.1.call-update) | async-done | bytes 4194320 | tf_op jit(solution)/shard_map/psum | solution.py:66
  293.0 59.8 %all-gather.24.cloned.1.call-done = bf16[2048,1536]{1,0:T(8,128)(2,1)} async-done(((bf16[256,1536]{1,0:T(8,128)(2,1)}), bf16[2048,1536]{1,0:T(8,128)(2,1)}) %all-gather.24.cloned.1.call-update) | async-done | bytes 6291472 | tf_op jit(solution)/shard_map/all_gather | solution.py:120
  352.8 8.5 fusion.83
  361.3 56.5 %all-gather.26.cloned.1.call-done = bf16[2048,1536]{1,0:T(8,128)(2,1)} async-done(((bf16[256,1536]{1,0:T(8,128)(2,1)}), bf16[2048,1536]{1,0:T(8,128)(2,1)}) %all-gather.26.cloned.1.call-update) | async-done | bytes 6291472 | tf_op jit(solution)/shard_map/all_gather | solution.py:121
  417.7 8.5 fusion.84
  426.2 56.8 %all-gather.28.cloned.1.call-done = bf16[1536,2048]{1,0:T(8,128)(2,1)} async-done(((bf16[1536,256]{1,0:T(8,128)(2,1)}), bf16[1536,2048]{1,0:T(8,128)(2,1)}) %all-gather.28.cloned.1.call-update) | async-done | bytes 6291472 | tf_op jit(solution)/shard_map/all_gather | solution.py:122
  483.0 9.8 multiply_convert_fusion.1
  492.9 7.3 fusion.86
  500.2 4.9 fusion.85
  505.2 5.0 convolution_add_fusion
  510.3 170.3 %all-reduce.18.cloned.1.call-done = (f32[512,2048]{1,0:T(8,128)}, f32[512,2048]{1,0:T(8,128)}) async-done(((f32[512,2048]{1,0:T(8,128)}, f32[512,2048]{1,0:T(8,128)}), (f32[512,2048]{1,0:T(8,128)}, f32[512,2048]{1,0:T(8,128)})) %all-reduce.18.cloned.1.call-update) | async-done | bytes 8388624 | tf_op jit(solution)/shard_map/psum | solution.py:66
  680.6 4.7 multiply_reduce_fusion
  685.3 6.6 subtract_add_fusion
  696.3 9.5 fusion.1
  705.7 11.6 fusion.3
  717.3 3.9 fusion.27
  721.4 10.0 fusion.20
  731.7 5.1 fusion.31
  740.9 4.8 convolution_convert_fusion.3
  745.8 8.2 convolution_convert_fusion.2
  754.1 8.2 convolution_convert_fusion.1
  770.1 40.8 %reduce-scatter.12.cloned.1.call-done = f32[512,256]{0,1:T(8,128)} async-done(((f32[2048,256]{0,1:T(8,128)}), f32[512,256]{0,1:T(8,128)}) %reduce-scatter.12.cloned.1.call-update) | async-done | bytes 524304 | tf_op jit(solution)/shard_map/reduce_scatter | solution.py:240
  813.6 4.3 add_convert_fusion
  818.0 8.2 convolution_convert_fusion
  831.6 29.7 %reduce-scatter.14.cloned.1.call-done = bf16[256,512]{1,0:T(8,128)(2,1)} async-done(((bf16[2048,512]{1,0:T(8,128)(2,1)}), bf16[256,512]{1,0:T(8,128)(2,1)}) %reduce-scatter.14.cloned.1.call-update) | async-done | bytes 262160 | tf_op jit(solution)/shard_map/reduce_scatter | solution.py:291
  863.2 48.6 %reduce-scatter.20.cloned.1.call-done = bf16[512,256]{1,0:T(8,128)(2,1)} async-done(((bf16[512,2048]{1,0:T(8,128)(2,1)}), bf16[512,256]{1,0:T(8,128)(2,1)}) %reduce-scatter.20.cloned.1.call-update) | async-done | bytes 262160 | tf_op jit(solution)/shard_map/reduce_scatter | solution.py:300
  913.6 127.4 %reduce-scatter.22.cloned.1.call-done = bf16[256,1536]{1,0:T(8,128)(2,1)} async-done(((bf16[2048,1536]{1,0:T(8,128)(2,1)}), bf16[256,1536]{1,0:T(8,128)(2,1)}) %reduce-scatter.22.cloned.1.call-update) | async-done | bytes 786448 | tf_op jit(solution)/shard_map/reduce_scatter | solution.py:303
  1043.4 128.1 %reduce-scatter.24.cloned.1.call-done = bf16[256,1536]{1,0:T(8,128)(2,1)} async-done(((bf16[2048,1536]{1,0:T(8,128)(2,1)}), bf16[256,1536]{1,0:T(8,128)(2,1)}) %reduce-scatter.24.cloned.1.call-update) | async-done | bytes 786448 | tf_op jit(solution)/shard_map/reduce_scatter | solution.py:306
  1174.0 70.6 %all-reduce.16.cloned.1.call-done = bf16[512,2048]{1,0:T(8,128)(2,1)} async-done(((bf16[512,2048]{1,0:T(8,128)(2,1)}), bf16[512,2048]{1,0:T(8,128)(2,1)}) %all-reduce.16.cloned.1.call-update) | async-done | bytes 2097168 | tf_op jit(solution)/shard_map/psum | solution.py:271
  1247.7 20.1 %all-reduce.7 = (bf16[2048]{0:T(1024)(128)(2,1)S(1)}, bf16[2048]{0:T(1024)(128)(2,1)S(1)}, bf16[128]{0:T(256)(128)(2,1)S(1)}, bf16[128]{0:T(256)(128)(2,1)S(1)}) all-reduce(bf16[2048]{0:T(1024)(128)(2,1)S(1)} %get-tuple-element.15, ...), channel_id=11, replica_groups=mesh['dp'=2,'ctx'=4,'tensor'=4] {'dp','ctx'}, use_global_device_ids=true, to_apply=%region_27.28.clone | all-reduce | flops 4352 | bytes 17408
  1268.0 108.0 %reduce-scatter.26.cloned.1.call-done = bf16[1536,256]{1,0:T(8,128)(2,1)} async-done(((bf16[1536,2048]{1,0:T(8,128)(2,1)}), bf16[1536,256]{1,0:T(8,128)(2,1)}) %reduce-scatter.26.cloned.1.call-update) | async-done | bytes 786448 | tf_op jit(solution)/shard_map/reduce_scatter | solution.py:309
  1378.4 9.8 all-reduce.9
  1389.2 25.4 %reduce-scatter.16.cloned.1.call-done = bf16[256,256]{1,0:T(8,128)(2,1)} async-done(((bf16[2048,256]{1,0:T(8,128)(2,1)}), bf16[256,256]{1,0:T(8,128)(2,1)}) %reduce-scatter.16.cloned.1.call-update) | async-done | bytes 131088 | tf_op jit(solution)/shard_map/reduce_scatter | solution.py:294
  1416.8 6.3 fusion.15
  1423.2 28.8 %reduce-scatter.18.cloned.1.call-done = bf16[256,256]{1,0:T(8,128)(2,1)} async-done(((bf16[2048,256]{1,0:T(8,128)(2,1)}), bf16[256,256]{1,0:T(8,128)(2,1)}) %reduce-scatter.18.cloned.1.call-update) | async-done | bytes 131088 | tf_op jit(solution)/shard_map/reduce_scatter | solution.py:297
  (231 shorter events, 75.0 us)
Async XLA Ops:
  7.2 27.4 %all-gather.12.cloned.1.call-start = ((), (), s32[]{:S(2)}) async-start(), calls=%async_computation.9 | async-start | bytes 1179648 | tf_op jit(solution)/shard_map/all_gather | solution.py:113
  7.9 51.2 %all-gather.16.cloned.1.call-start = ((), (), s32[]{:S(2)}) async-start(), calls=%async_computation.11 | async-start | bytes 1179648 | tf_op jit(solution)/shard_map/all_gather | solution.py:112
  8.7 79.2 %all-gather.14.cloned.1.call-start = ((), (), s32[]{:S(2)}) async-start(), calls=%async_computation.10 | async-start | bytes 1310720 | tf_op jit(solution)/shard_map/all_gather | solution.py:168
  27.3 90.6 %copy-start.21 = (f32[8,1,256]{2,1,0:T(1,128)}, f32[8,1,256]{2,1,0:T(1,128)S(1)}, u32[]{:S(2)}) copy-start(f32[8,1,256]{2,1,0:T(1,128)S(1)} %convert_element_type.255) | copy-start | bytes 24580
  27.3 11.3 copy-start.33
  27.3 12.5 copy-start.35
  27.3 12.8 copy-start.36
  27.3 29.3 %copy-start.34 = (s32[1,13]{1,0:T(1,128)S(1)}, s32[1,13]{1,0:T(1,128)}, u32[]{:S(2)}) copy-start(s32[1,13]{1,0:T(1,128)} %param.16) | copy-start | bytes 160
  27.3 29.5 %copy-start.37 = (s32[1,13]{1,0:T(1,128)S(1)}, s32[1,13]{1,0:T(1,128)}, u32[]{:S(2)}) copy-start(s32[1,13]{1,0:T(1,128)} %param.17) | copy-start | bytes 160
  27.4 31.8 %copy-start.3 = (bf16[512,2048]{1,0:T(8,128)(2,1)S(1)}, bf16[512,2048]{1,0:T(8,128)(2,1)}, u32[]{:S(2)}) copy-start(bf16[512,2048]{1,0:T(8,128)(2,1)} %param.15) | copy-start | bytes 6291460
  29.6 88.3 %copy-start.27 = (f32[512]{0:T(512)}, f32[512]{0:T(512)S(1)}, u32[]{:S(2)}) copy-start(f32[512]{0:T(512)S(1)} %add_rsqrt_fusion.3) | copy-start | bytes 6148
  37.9 80.0 %all-gather.20.cloned.1.call-start = ((), (), s32[]{:S(2)}) async-start(), calls=%async_computation.13 | async-start | bytes 2359296 | tf_op jit(solution)/shard_map/all_gather | solution.py:111
  38.5 108.8 %all-gather.18.cloned.1.call-start = ((), (), s32[]{:S(2)}) async-start(), calls=%async_computation.12 | async-start | bytes 1310720 | tf_op jit(solution)/shard_map/all_gather | solution.py:167
  59.1 63.0 %copy-start.10 = (f32[512,64]{0,1:T(8,128)}, f32[512,64]{0,1:T(8,128)S(1)}, u32[]{:S(2)}) copy-start(f32[512,64]{0,1:T(8,128)S(1)} %get-tuple-element.50) | copy-start | bytes 393220
  59.1 63.0 %copy-start.12 = (f32[512,64]{0,1:T(8,128)}, f32[512,64]{0,1:T(8,128)S(1)}, u32[]{:S(2)}) copy-start(f32[512,64]{0,1:T(8,128)S(1)} %get-tuple-element.51) | copy-start | bytes 393220
  63.1 115.6 %all-gather.22.cloned.1.call-start = ((), (), s32[]{:S(2)}) async-start(), calls=%async_computation.14 | async-start | bytes 2359296 | tf_op jit(solution)/shard_map/all_gather | solution.py:114
  63.7 222.7 %all-reduce.14.cloned.1.call-start = ((), (), s32[]{:S(2)}) async-start(), calls=%async_computation.15 | async-start | bytes 8388608 | tf_op jit(solution)/shard_map/psum | solution.py:66
  64.2 56.7 %copy-start.29 = (f32[128]{0:T(128)}, f32[128]{0:T(128)S(1)}, u32[]{:S(2)}) copy-start(f32[128]{0:T(128)S(1)} %convert_element_type.203) | copy-start | bytes 1540
  122.8 38.3 %copy-start.14 = (bf16[512,4,64]{2,0,1:T(8,128)(2,1)}, bf16[512,4,64]{2,0,1:T(8,128)(2,1)S(1)}, u32[]{:S(2)}) copy-start(bf16[512,4,64]{2,0,1:T(8,128)(2,1)S(1)} %copy.66) | copy-start | bytes 786436
  168.8 14.8 %copy-start.18 = (bf16[2,128,2,512]{3,1,2,0:T(8,128)(2,1)}, bf16[2,128,2,512]{3,1,2,0:T(8,128)(2,1)S(1)}, u32[]{:S(2)}) copy-start(bf16[2,128,2,512]{3,1,2,0:T(8,128)(2,1)S(1)} %fusion.32) | copy-start | bytes 1572868
  183.7 169.1 %all-gather.24.cloned.1.call-start = ((), (), s32[]{:S(2)}) async-start(), calls=%async_computation.16 | async-start | bytes 7077888 | tf_op jit(solution)/shard_map/all_gather | solution.py:120
  184.4 233.3 %all-gather.26.cloned.1.call-start = ((), (), s32[]{:S(2)}) async-start(), calls=%async_computation.17 | async-start | bytes 7077888 | tf_op jit(solution)/shard_map/all_gather | solution.py:121
  185.1 297.8 %all-gather.28.cloned.1.call-start = ((), (), s32[]{:S(2)}) async-start(), calls=%async_computation.18 | async-start | bytes 7077888 | tf_op jit(solution)/shard_map/all_gather | solution.py:122
  185.7 494.9 %all-reduce.18.cloned.1.call-start = ((), (), s32[]{:S(2)}) async-start(), calls=%async_computation.29 | async-start | bytes 16777216 | tf_op jit(solution)/shard_map/psum | solution.py:66
  483.0 17.2 %slice-start.6 = ((s8[6291456]{0:T(1024)(128)(4,1)}), s8[4194304]{0:T(1024)(128)(4,1)S(1)}, s32[]{:S(2)}) async-start(s8[6291456]{0:T(1024)(128)(4,1)} %bitcast.248), calls=%async_computation.36 | async-start | bytes 8388608
  483.0 22.2 %slice-start.4 = ((s8[6291456]{0:T(1024)(128)(4,1)}), s8[2097152]{0:T(1024)(128)(4,1)S(1)}, s32[]{:S(2)}) async-start(s8[6291456]{0:T(1024)(128)(4,1)} %bitcast.246), calls=%async_computation.34 | async-start | bytes 4194304
  492.8 7.3 copy-start.42
  492.8 7.3 copy-start.41
  492.9 12.3 copy-start.40
  492.9 7.3 slice-start.7
  492.9 12.3 slice-start.5
  510.2 255.5 %reduce-scatter.10.cloned.1.call-start = ((), (), s32[]{:S(2)}) async-start(), calls=%async_computation.19 | async-start | bytes 2621440 | tf_op jit(solution)/shard_map/reduce_scatter | solution.py:234
  680.6 15.6 %slice-start = ((s8[16777216]{0:T(1024)(128)(4,1)}), s8[4194304]{0:T(1024)(128)(4,1)S(1)}, s32[]{:S(2)}) async-start(s8[16777216]{0:T(1024)(128)(4,1)} %bitcast.216), calls=%async_computation.30 | async-start | bytes 8388608
  685.3 8.8 copy-start.16
  685.3 10.8 slice-start.1
  685.3 10.8 slice-start.2
  685.3 11.0 slice-start.3
  705.7 11.6 copy-start.15
  721.3 10.4 copy-start.30
  721.3 89.6 %reduce-scatter.12.cloned.1.call-start = ((), (), s32[]{:S(2)}) async-start(), calls=%async_computation.20 | async-start | bytes 2621440 | tf_op jit(solution)/shard_map/reduce_scatter | solution.py:240
  731.4 130.0 %reduce-scatter.14.cloned.1.call-start = ((), (), s32[]{:S(2)}) async-start(), calls=%async_computation.22 | async-start | bytes 2359296 | tf_op jit(solution)/shard_map/reduce_scatter | solution.py:291
  740.9 170.9 %reduce-scatter.20.cloned.1.call-start = ((), (), s32[]{:S(2)}) async-start(), calls=%async_computation.25 | async-start | bytes 2359296 | tf_op jit(solution)/shard_map/reduce_scatter | solution.py:300
  745.8 295.2 %reduce-scatter.22.cloned.1.call-start = ((), (), s32[]{:S(2)}) async-start(), calls=%async_computation.26 | async-start | bytes 7077888 | tf_op jit(solution)/shard_map/reduce_scatter | solution.py:303
  754.1 417.5 %reduce-scatter.24.cloned.1.call-start = ((), (), s32[]{:S(2)}) async-start(), calls=%async_computation.27 | async-start | bytes 7077888 | tf_op jit(solution)/shard_map/reduce_scatter | solution.py:306
  762.3 482.3 %all-reduce.16.cloned.1.call-start = ((), (), s32[]{:S(2)}) async-start(), calls=%async_computation.21 | async-start | bytes 4194304 | tf_op jit(solution)/shard_map/psum | solution.py:271
  817.9 558.1 %reduce-scatter.26.cloned.1.call-start = ((), (), s32[]{:S(2)}) async-start(), calls=%async_computation.28 | async-start | bytes 7077888 | tf_op jit(solution)/shard_map/reduce_scatter | solution.py:309
  826.2 588.4 %reduce-scatter.16.cloned.1.call-start = ((), (), s32[]{:S(2)}) async-start(), calls=%async_computation.23 | async-start | bytes 1179648 | tf_op jit(solution)/shard_map/reduce_scatter | solution.py:294
  828.2 623.7 %reduce-scatter.18.cloned.1.call-start = ((), (), s32[]{:S(2)}) async-start(), calls=%async_computation.24 | async-start | bytes 1179648 | tf_op jit(solution)/shard_map/reduce_scatter | solution.py:297
  (24 other events, 69.1 us)
Sparse Core Ops, SparseCore 0:
  9.6 24.9 all-gather.11
  36.2 22.2 all-gather.15
  60.6 27.1 all-gather.13
  89.3 28.5 all-gather.19
  119.9 27.3 all-gather.17
  148.7 29.9 all-gather.21
  183.8 102.6 all-reduce.13
  288.0 64.6 all-gather.23
  354.4 63.3 all-gather.25
  419.2 63.7 all-gather.27
  510.3 170.2 all-reduce.17
  721.4 44.2 reduce-scatter.9
  768.0 42.8 reduce-scatter.11
  813.0 48.2 reduce-scatter.13
  863.5 48.2 reduce-scatter.19
  914.0 126.9 reduce-scatter.21
  1043.1 128.3 reduce-scatter.23
  1174.5 70.0 all-reduce.15
  1246.9 129.0 reduce-scatter.25
  1378.1 36.3 reduce-scatter.15
  1416.8 35.0 reduce-scatter.17
where the time goes:
time: 1470 us; the launch traced here: 1460 us
  waiting for transfers between devices  1130 us (77%)
  matrix products  160 us (11%)
  blocking collectives  80.5 us (5%)
  other arithmetic  60.2 us (4%)
  between operations  17.6 us (1%)
    psum x2, waiting for transfers between devices, tensor_sum(): return lax.psum(values, 'tensor')  255 us
    reduce_scatter x1, waiting for transfers between devices, on_device(): lax.psum_scatter(grad_up.astype(jnp.bfloat16), ('dp', 'ctx'), scatter_dim...  128 us
    reduce_scatter x1, waiting for transfers between devices, on_device(): lax.psum_scatter(grad_gate.astype(jnp.bfloat16), ('dp', 'ctx'), scatter_d...  127 us
    reduce_scatter x1, waiting for transfers between devices, on_device(): lax.psum_scatter(grad_down.astype(jnp.bfloat16), ('dp', 'ctx'), scatter_d...  108 us
    psum x1, waiting for transfers between devices, on_device(): lax.psum(partial_value.astype(jnp.bfloat16), 'tensor').astype(jnp.float32)  70.6 us
    all_gather x1, waiting for transfers between devices, on_device(): lax.all_gather(w_gate, ('dp', 'ctx'), axis=0, tiled=True)  59.8 us
    all_gather x1, waiting for transfers between devices, on_device(): lax.all_gather(w_down, ('dp', 'ctx'), axis=1, tiled=True)  56.8 us
    all_gather x1, waiting for transfers between devices, on_device(): lax.all_gather(w_up, ('dp', 'ctx'), axis=0, tiled=True)  56.5 us
  transfers between devices with their start and end apart: 21, of which 20 were waited for; matrix products, arithmetic and copies ran while one was open for 11% of the time, Pallas kernels for 0%

commit v1 on v0

--- a/solution.py
+++ b/solution.py
@@ -8,6 +8,32 @@
 EPS = 1e-06
 THETA = 1000000.0
 PRECISE = lax.Precision.HIGHEST
+
+
+def supply_all_axis_part(s0, array_dim):
+    s0 = jnp.moveaxis(s0, 0, array_dim)
+    arr_next = s0.shape
+    return s0.reshape(
+        *arr_next[:array_dim],
+        arr_next[array_dim] * arr_next[array_dim + 1],
+        *arr_next[array_dim + 2 :]
+    )
+
+
+def _do_paths(arr, dimension_no, chip_axis):
+    total_devices = jax.lax.axis_size(chip_axis)
+    in_order = [(j0, (j0 + 1) % total_devices) for j0 in range(total_devices)]
+    all_blocks = [(m, dev_j) for dev_j, m in in_order]
+    extra, d_next = ([], [])
+    for t in [*range(total_devices - 1)]:
+        if t % 2 == 0:
+            extra.append(jax.lax.ppermute(extra[-1] if extra else arr, chip_axis, in_order))
+        else:
+            d_next.append(jax.lax.ppermute(d_next[-1] if d_next else arr, chip_axis, all_blocks))
+    b_now = jnp.stack([*extra[::-1], arr, *d_next], axis=0)
+    item_now = jax.lax.axis_index(chip_axis) - len(extra)
+    b_now = b_now[(jnp.arange(total_devices) - item_now) % total_devices]
+    return supply_all_axis_part(b_now, dimension_no)
 
 
 def norm_rows(values, gain_vec):
@@ -117,7 +143,7 @@
         lax.all_gather(gain_key, ("dp", "ctx"), axis=0, tiled=True),
     )
     mlp_set = (
-        lax.all_gather(w_gate, ("dp", "ctx"), axis=0, tiled=True),
+        _do_paths(w_gate, 0, ("dp", "ctx")),
         lax.all_gather(w_up, ("dp", "ctx"), axis=0, tiled=True),
         lax.all_gather(w_down, ("dp", "ctx"), axis=1, tiled=True),
         lax.all_gather(gain_mlp, ("dp", "ctx"), axis=0, tiled=True),

time: 1470 us -> 1420 us (0.966)
  waiting for transfers between devices: 1130 us -> 1030 us
  blocking collectives: 80.5 us -> 105 us
  local copies, waits for them, and re-layouts: 14.5 us -> 34.4 us
    ppermute x0 -> x7, waiting for transfers between devices: none -> 108 us  [the longest x3 57.4 us: _do_paths(): jax.lax.ppermute(d_next[-1] if d_next else arr, chip_axis, all_blocks)]
    psum x2, waiting for transfers between devices: 255 us -> 170 us  [tensor_sum(): return lax.psum(values, 'tensor')]
    all_gather x1 -> x0, waiting for transfers between devices: 59.8 us -> none  [on_device(): lax.all_gather(w_gate, ('dp', 'ctx'), axis=0, tiled=True)]
    all_gather x1, waiting for transfers between devices: 56.5 us -> 0.01 us  [on_device(): lax.all_gather(w_up, ('dp', 'ctx'), axis=0, tiled=True)]
    all_gather x1, blocking collectives: 16.4 us -> 41.2 us  [on_device(): lax.all_gather(gain_mlp, ('dp', 'ctx'), axis=0, tiled=True)]
  transfers between devices with their start and end apart: 21 -> 27, of which waited for: 20 -> 22; matrix products, arithmetic and copies ran while one was open for 11% -> 12% of each run, Pallas kernels for 0% -> 0%
where the time goes in v1:
time: 1420 us; the launch traced here: 1410 us
  waiting for transfers between devices  1030 us (73%)
  matrix products  153 us (11%)
  blocking collectives  105 us (7%)
  other arithmetic  60 us (4%)
  local copies, waits for them, and re-layouts  34.4 us (2%)
  between operations  17.7 us (1%)
  starting transfers between devices  14.6 us (1%)
    psum x2, waiting for transfers between devices, tensor_sum(): return lax.psum(values, 'tensor')  170 us
    reduce_scatter x1, waiting for transfers between devices, on_device(): lax.psum_scatter(grad_up.astype(jnp.bfloat16), ('dp', 'ctx'), scatter_dim...  128 us
    reduce_scatter x1, waiting for transfers between devices, on_device(): lax.psum_scatter(grad_gate.astype(jnp.bfloat16), ('dp', 'ctx'), scatter_d...  127 us
    reduce_scatter x1, waiting for transfers between devices, on_device(): lax.psum_scatter(grad_down.astype(jnp.bfloat16), ('dp', 'ctx'), scatter_d...  108 us
    psum x1, waiting for transfers between devices, on_device(): lax.psum(partial_value.astype(jnp.bfloat16), 'tensor').astype(jnp.float32)  70.6 us
    ppermute x3, waiting for transfers between devices, _do_paths(): jax.lax.ppermute(d_next[-1] if d_next else arr, chip_axis, all_blocks)  57.4 us
    all_gather x1, waiting for transfers between devices, on_device(): lax.all_gather(w_down, ('dp', 'ctx'), axis=1, tiled=True)  52.3 us
    ppermute x4, waiting for transfers between devices, _do_paths(): jax.lax.ppermute(extra[-1] if extra else arr, chip_axis, in_order)  50.6 us
  transfers between devices with their start and end apart: 27, of which 22 were waited for; matrix products, arithmetic and copies ran while one was open for 12% of the time, Pallas kernels for 0%

profile of v1, /device:TPU:0, one launch (start us, length us, event | category | flops | bytes accessed | tf_op | source)
XLA Modules:
  0.0 1413.9 jit_solution(9243245424056611303)
XLA Ops:
  9.4 17.9 %all-gather = bf16[8,1,256]{2,1,0:T(2,128)(2,1)S(1)} all-gather(bf16[1,1,256]{2,1,0:T(2,128)(2,1)S(1)} %reshape.304), channel_id=1, replica_groups=mesh['dp'=2,'ctx'=4,'tensor'=4] {'dp','ctx'}, dimensions={0}, use_global_device_ids=true | all-gather | bytes 4608 | tf_op jit(solution)/shard_map/all_gather | solution.py:141
  29.6 4.9 all-gather.11.cloned.1.call-done
  40.3 16.3 %all-reduce.8 = (bf16[128]{0:T(256)(128)(2,1)S(1)}, bf16[128]{0:T(256)(128)(2,1)S(1)}) all-reduce(bf16[128]{0:T(256)(128)(2,1)S(1)} %dynamic-update-slice, bf16[128]{0:T(256)(128)(2,1)S(1)} %dynamic-update-slice.1), channel_id=1, replica_groups=mesh['dp'=2,'ctx'=4,'tensor'=4] {'dp','ctx'}, use_global_device_ids=true, to_apply=%add | all-reduce | flops 256 | bytes 1024
  70.3 17.5 %all-gather.13.cloned.1.call-done = bf16[2048,256]{1,0:T(8,128)(2,1)} async-done(((bf16[512,256]{1,0:T(8,128)(2,1)}), bf16[2048,256]{1,0:T(8,128)(2,1)}) %all-gather.13.cloned.1.call-update) | async-done | bytes 1048592 | tf_op jit(solution)/shard_map/all_gather | solution.py:194
  90.2 27.7 %all-gather.19.cloned.1.call-done = bf16[2048,512]{1,0:T(8,128)(2,1)} async-done(((bf16[256,512]{1,0:T(8,128)(2,1)}), bf16[2048,512]{1,0:T(8,128)(2,1)}) %all-gather.19.cloned.1.call-update) | async-done | bytes 2097168 | tf_op jit(solution)/shard_map/all_gather | solution.py:137
  122.8 24.5 %all-gather.17.cloned.1.call-done = bf16[2048,256]{0,1:T(8,128)(2,1)} async-done(((bf16[512,256]{0,1:T(8,128)(2,1)}), bf16[2048,256]{0,1:T(8,128)(2,1)}) %all-gather.17.cloned.1.call-update) | async-done | bytes 1048592 | tf_op jit(solution)/shard_map/all_gather | solution.py:193
  147.3 14.0 fusion.83
  161.2 7.6 fusion.32
  168.9 9.8 all-gather.21.cloned.1.call-done
  178.7 4.9 fusion.84
  188.5 18.0 %collective-permute-done = bf16[256,1536]{1,0:T(8,128)(2,1)S(1)} collective-permute-done((bf16[256,1536]{1,0:T(8,128)(2,1)S(1)}, bf16[256,1536]{1,0:T(8,128)(2,1)S(1)}, u32[]{:S(2)}, u32[]{:S(2)}) %collective-permute-start) | collective-permute-done | bytes 786464 | tf_op jit(solution)/shard_map/ppermute | solution.py:30
  210.0 17.8 %collective-permute-done.1 = bf16[256,1536]{1,0:T(8,128)(2,1)S(1)} collective-permute-done((bf16[256,1536]{1,0:T(8,128)(2,1)S(1)}, bf16[256,1536]{1,0:T(8,128)(2,1)S(1)}, u32[]{:S(2)}, u32[]{:S(2)}) %collective-permute-start.1) | collective-permute-done | bytes 786464 | tf_op jit(solution)/shard_map/ppermute | solution.py:30
  228.6 15.2 %collective-permute-done.4 = bf16[256,1536]{1,0:T(8,128)(2,1)} collective-permute-done((bf16[256,1536]{1,0:T(8,128)(2,1)S(1)}, bf16[256,1536]{1,0:T(8,128)(2,1)}, u32[]{:S(2)}, u32[]{:S(2)}) %collective-permute-start.4) | collective-permute-done | bytes 786464 | tf_op jit(solution)/shard_map/ppermute | solution.py:32
  246.8 14.9 %collective-permute-done.2 = bf16[256,1536]{1,0:T(8,128)(2,1)} collective-permute-done((bf16[256,1536]{1,0:T(8,128)(2,1)S(1)}, bf16[256,1536]{1,0:T(8,128)(2,1)}, u32[]{:S(2)}, u32[]{:S(2)}) %collective-permute-start.2) | collective-permute-done | bytes 786464 | tf_op jit(solution)/shard_map/ppermute | solution.py:30
  262.9 41.2 %all-gather.1 = bf16[8,1,256]{2,1,0:T(2,128)(2,1)S(1)} all-gather(bf16[1,1,256]{2,1,0:T(2,128)(2,1)S(1)} %reshape.306), channel_id=1, replica_groups=mesh['dp'=2,'ctx'=4,'tensor'=4] {'dp','ctx'}, dimensions={0}, use_global_device_ids=true | all-gather | bytes 4608 | tf_op jit(solution)/shard_map/all_gather | solution.py:149
  317.7 42.2 %collective-permute-done.6 = bf16[256,1536]{1,0:T(8,128)(2,1)S(1)} collective-permute-done((bf16[256,1536]{1,0:T(8,128)(2,1)}, bf16[256,1536]{1,0:T(8,128)(2,1)S(1)}, u32[]{:S(2)}, u32[]{:S(2)}) %collective-permute-start.6) | collective-permute-done | bytes 786464 | tf_op jit(solution)/shard_map/ppermute | solution.py:32
  360.8 6.4 gather_fusion
  373.9 8.8 fusion.85
  382.6 52.3 %all-gather.25.cloned.1.call-done = bf16[1536,2048]{1,0:T(8,128)(2,1)} async-done(((bf16[1536,256]{1,0:T(8,128)(2,1)}), bf16[1536,2048]{1,0:T(8,128)(2,1)}) %all-gather.25.cloned.1.call-update) | async-done | bytes 6291472 | tf_op jit(solution)/shard_map/all_gather | solution.py:148
  434.9 6.4 fusion.87
  441.4 8.5 multiply_convert_fusion.2
  453.4 5.0 convolution_add_fusion
  458.4 4.9 fusion.86
  463.6 170.2 %all-reduce.18.cloned.1.call-done = (f32[512,2048]{1,0:T(8,128)}, f32[512,2048]{1,0:T(8,128)}) async-done(((f32[512,2048]{1,0:T(8,128)}, f32[512,2048]{1,0:T(8,128)}), (f32[512,2048]{1,0:T(8,128)}, f32[512,2048]{1,0:T(8,128)})) %all-reduce.18.cloned.1.call-update) | async-done | bytes 8388624 | tf_op jit(solution)/shard_map/psum | solution.py:92
  633.8 4.7 multiply_reduce_fusion
  638.5 6.3 subtract_add_fusion
  649.5 9.5 fusion.1
  658.9 11.6 fusion.3
  670.5 3.9 fusion.27
  674.6 10.0 fusion.20
  684.9 5.1 fusion.31
  694.1 4.8 convolution_convert_fusion.3
  699.0 8.2 convolution_convert_fusion.2
  707.3 8.2 convolution_convert_fusion.1
  723.4 40.6 %reduce-scatter.12.cloned.1.call-done = f32[512,256]{0,1:T(8,128)} async-done(((f32[2048,256]{0,1:T(8,128)}), f32[512,256]{0,1:T(8,128)}) %reduce-scatter.12.cloned.1.call-update) | async-done | bytes 524304 | tf_op jit(solution)/shard_map/reduce_scatter | solution.py:266
  766.7 4.4 add_convert_fusion
  771.1 8.2 convolution_convert_fusion
  784.8 29.8 %reduce-scatter.14.cloned.1.call-done = bf16[256,512]{1,0:T(8,128)(2,1)} async-done(((bf16[2048,512]{1,0:T(8,128)(2,1)}), bf16[256,512]{1,0:T(8,128)(2,1)}) %reduce-scatter.14.cloned.1.call-update) | async-done | bytes 262160 | tf_op jit(solution)/shard_map/reduce_scatter | solution.py:317
  816.4 48.6 %reduce-scatter.20.cloned.1.call-done = bf16[512,256]{1,0:T(8,128)(2,1)} async-done(((bf16[512,2048]{1,0:T(8,128)(2,1)}), bf16[512,256]{1,0:T(8,128)(2,1)}) %reduce-scatter.20.cloned.1.call-update) | async-done | bytes 262160 | tf_op jit(solution)/shard_map/reduce_scatter | solution.py:326
  866.8 127.4 %reduce-scatter.22.cloned.1.call-done = bf16[256,1536]{1,0:T(8,128)(2,1)} async-done(((bf16[2048,1536]{1,0:T(8,128)(2,1)}), bf16[256,1536]{1,0:T(8,128)(2,1)}) %reduce-scatter.22.cloned.1.call-update) | async-done | bytes 786448 | tf_op jit(solution)/shard_map/reduce_scatter | solution.py:329
  996.7 128.1 %reduce-scatter.24.cloned.1.call-done = bf16[256,1536]{1,0:T(8,128)(2,1)} async-done(((bf16[2048,1536]{1,0:T(8,128)(2,1)}), bf16[256,1536]{1,0:T(8,128)(2,1)}) %reduce-scatter.24.cloned.1.call-update) | async-done | bytes 786448 | tf_op jit(solution)/shard_map/reduce_scatter | solution.py:332
  1127.2 70.6 %all-reduce.16.cloned.1.call-done = bf16[512,2048]{1,0:T(8,128)(2,1)} async-done(((bf16[512,2048]{1,0:T(8,128)(2,1)}), bf16[512,2048]{1,0:T(8,128)(2,1)}) %all-reduce.16.cloned.1.call-update) | async-done | bytes 2097168 | tf_op jit(solution)/shard_map/psum | solution.py:297
  1201.0 20.0 %all-reduce.7 = (bf16[2048]{0:T(1024)(128)(2,1)S(1)}, bf16[2048]{0:T(1024)(128)(2,1)S(1)}, bf16[128]{0:T(256)(128)(2,1)S(1)}, bf16[128]{0:T(256)(128)(2,1)S(1)}) all-reduce(bf16[2048]{0:T(1024)(128)(2,1)S(1)} %get-tuple-element.15, ...), channel_id=11, replica_groups=mesh['dp'=2,'ctx'=4,'tensor'=4] {'dp','ctx'}, use_global_device_ids=true, to_apply=%region_27.28.clone | all-reduce | flops 4352 | bytes 17408
  1221.1 108.0 %reduce-scatter.26.cloned.1.call-done = bf16[1536,256]{1,0:T(8,128)(2,1)} async-done(((bf16[1536,2048]{1,0:T(8,128)(2,1)}), bf16[1536,256]{1,0:T(8,128)(2,1)}) %reduce-scatter.26.cloned.1.call-update) | async-done | bytes 786448 | tf_op jit(solution)/shard_map/reduce_scatter | solution.py:335
  1331.5 9.8 all-reduce.9
  1342.3 25.6 %reduce-scatter.16.cloned.1.call-done = bf16[256,256]{1,0:T(8,128)(2,1)} async-done(((bf16[2048,256]{1,0:T(8,128)(2,1)}), bf16[256,256]{1,0:T(8,128)(2,1)}) %reduce-scatter.16.cloned.1.call-update) | async-done | bytes 131088 | tf_op jit(solution)/shard_map/reduce_scatter | solution.py:320
  1370.1 6.3 fusion.15
  1376.5 28.6 %reduce-scatter.18.cloned.1.call-done = bf16[256,256]{1,0:T(8,128)(2,1)} async-done(((bf16[2048,256]{1,0:T(8,128)(2,1)}), bf16[256,256]{1,0:T(8,128)(2,1)}) %reduce-scatter.18.cloned.1.call-update) | async-done | bytes 131088 | tf_op jit(solution)/shard_map/reduce_scatter | solution.py:323
  (270 shorter events, 111.3 us)
Async XLA Ops:
  7.2 27.4 %all-gather.11.cloned.1.call-start = ((), (), s32[]{:S(2)}) async-start(), calls=%async_computation.9 | async-start | bytes 1179648 | tf_op jit(solution)/shard_map/all_gather | solution.py:139
  7.9 51.2 %all-gather.15.cloned.1.call-start = ((), (), s32[]{:S(2)}) async-start(), calls=%async_computation.11 | async-start | bytes 1179648 | tf_op jit(solution)/shard_map/all_gather | solution.py:138
  8.7 79.2 %all-gather.13.cloned.1.call-start = ((), (), s32[]{:S(2)}) async-start(), calls=%async_computation.10 | async-start | bytes 1310720 | tf_op jit(solution)/shard_map/all_gather | solution.py:194
  27.3 90.6 %copy-start.26 = (f32[8,1,256]{2,1,0:T(1,128)}, f32[8,1,256]{2,1,0:T(1,128)S(1)}, u32[]{:S(2)}) copy-start(f32[8,1,256]{2,1,0:T(1,128)S(1)} %convert_element_type.255) | copy-start | bytes 24580
  27.3 11.3 copy-start.38
  27.3 12.5 copy-start.40
  27.3 12.8 copy-start.41
  27.3 29.3 %copy-start.39 = (s32[1,13]{1,0:T(1,128)S(1)}, s32[1,13]{1,0:T(1,128)}, u32[]{:S(2)}) copy-start(s32[1,13]{1,0:T(1,128)} %param.16) | copy-start | bytes 160
  27.3 29.5 %copy-start.42 = (s32[1,13]{1,0:T(1,128)S(1)}, s32[1,13]{1,0:T(1,128)}, u32[]{:S(2)}) copy-start(s32[1,13]{1,0:T(1,128)} %param.17) | copy-start | bytes 160
  27.4 31.8 %copy-start.3 = (bf16[512,2048]{1,0:T(8,128)(2,1)S(1)}, bf16[512,2048]{1,0:T(8,128)(2,1)}, u32[]{:S(2)}) copy-start(bf16[512,2048]{1,0:T(8,128)(2,1)} %param.15) | copy-start | bytes 6291460
  29.6 88.3 %copy-start.32 = (f32[512]{0:T(512)}, f32[512]{0:T(512)S(1)}, u32[]{:S(2)}) copy-start(f32[512]{0:T(512)S(1)} %add_rsqrt_fusion.3) | copy-start | bytes 6148
  37.9 80.0 %all-gather.19.cloned.1.call-start = ((), (), s32[]{:S(2)}) async-start(), calls=%async_computation.13 | async-start | bytes 2359296 | tf_op jit(solution)/shard_map/all_gather | solution.py:137
  38.5 108.8 %all-gather.17.cloned.1.call-start = ((), (), s32[]{:S(2)}) async-start(), calls=%async_computation.12 | async-start | bytes 1310720 | tf_op jit(solution)/shard_map/all_gather | solution.py:193
  59.1 62.9 %copy-start.10 = (f32[512,64]{0,1:T(8,128)}, f32[512,64]{0,1:T(8,128)S(1)}, u32[]{:S(2)}) copy-start(f32[512,64]{0,1:T(8,128)S(1)} %get-tuple-element.50) | copy-start | bytes 393220
  59.1 62.9 %copy-start.12 = (f32[512,64]{0,1:T(8,128)}, f32[512,64]{0,1:T(8,128)S(1)}, u32[]{:S(2)}) copy-start(f32[512,64]{0,1:T(8,128)S(1)} %get-tuple-element.51) | copy-start | bytes 393220
  63.1 115.6 %all-gather.21.cloned.1.call-start = ((), (), s32[]{:S(2)}) async-start(), calls=%async_computation.14 | async-start | bytes 2359296 | tf_op jit(solution)/shard_map/all_gather | solution.py:140
  63.7 303.5 %all-reduce.14.cloned.1.call-start = ((), (), s32[]{:S(2)}) async-start(), calls=%async_computation.15 | async-start | bytes 8388608 | tf_op jit(solution)/shard_map/psum | solution.py:92
  64.2 56.7 %copy-start.34 = (f32[128]{0:T(128)}, f32[128]{0:T(128)S(1)}, u32[]{:S(2)}) copy-start(f32[128]{0:T(128)S(1)} %convert_element_type.203) | copy-start | bytes 1540
  122.8 38.4 %copy-start.15 = (bf16[512,4,64]{2,0,1:T(8,128)(2,1)}, bf16[512,4,64]{2,0,1:T(8,128)(2,1)S(1)}, u32[]{:S(2)}) copy-start(bf16[512,4,64]{2,0,1:T(8,128)(2,1)S(1)} %copy.66) | copy-start | bytes 786436
  183.6 79.2 %copy-start.43 = (bf16[256]{0:T(256)(128)(2,1)S(1)}, bf16[256]{0:T(256)(128)(2,1)}, u32[]{:S(2)}) copy-start(bf16[256]{0:T(256)(128)(2,1)} %param.26) | copy-start | bytes 1540
  183.7 190.2 %all-gather.23.cloned.1.call-start = ((), (), s32[]{:S(2)}) async-start(), calls=%async_computation.16 | async-start | bytes 7077888 | tf_op jit(solution)/shard_map/all_gather | solution.py:147
  184.4 250.5 %all-gather.25.cloned.1.call-start = ((), (), s32[]{:S(2)}) async-start(), calls=%async_computation.17 | async-start | bytes 7077888 | tf_op jit(solution)/shard_map/all_gather | solution.py:148
  185.1 448.6 %all-reduce.18.cloned.1.call-start = ((), (), s32[]{:S(2)}) async-start(), calls=%async_computation.28 | async-start | bytes 16777216 | tf_op jit(solution)/shard_map/psum | solution.py:92
  185.2 21.3 %collective-permute-start = (bf16[256,1536]{1,0:T(8,128)(2,1)S(1)}, bf16[256,1536]{1,0:T(8,128)(2,1)S(1)}, u32[]{:S(2)}, u32[]{:S(2)}) collective-permute-start(bf16[256,1536]{1,0:T(8,128)(2,1)S(1)} %copy-done.19), channel_id=1, source_target_pairs={{0,4},{4,8},{8,12},{12,16},{16,20},{20,24},{24,28},{28,0},{1,5},{5... | collective-permute-start | bytes 2359304 | tf_op jit(solution)/shard_map/ppermute | solution.py:30
  206.5 37.3 %copy-start.20 = (bf16[256,1536]{1,0:T(8,128)(2,1)}, bf16[256,1536]{1,0:T(8,128)(2,1)S(1)}, u32[]{:S(2)}) copy-start(bf16[256,1536]{1,0:T(8,128)(2,1)S(1)} %collective-permute-done) | copy-start | bytes 2359300
  206.5 21.3 %collective-permute-start.1 = (bf16[256,1536]{1,0:T(8,128)(2,1)S(1)}, bf16[256,1536]{1,0:T(8,128)(2,1)S(1)}, u32[]{:S(2)}, u32[]{:S(2)}) collective-permute-start(bf16[256,1536]{1,0:T(8,128)(2,1)S(1)} %collective-permute-done), channel_id=1, source_target_pairs={{0,4},{4,8},{8,12},{12,16},{16,20},{20,24},{24,28},{28,0},{1,5},{5... | collective-permute-start | bytes 2359304 | tf_op jit(solution)/shard_map/ppermute | solution.py:30
  208.2 35.6 %collective-permute-start.4 = (bf16[256,1536]{1,0:T(8,128)(2,1)S(1)}, bf16[256,1536]{1,0:T(8,128)(2,1)}, u32[]{:S(2)}, u32[]{:S(2)}) collective-permute-start(bf16[256,1536]{1,0:T(8,128)(2,1)S(1)} %copy-done.19), channel_id=1, source_target_pairs={{4,0},{8,4},{12,8},{16,12},{20,16},{24,20},{28,24},{0,28},{5,1},{9... | collective-permute-start | bytes 2359304 | tf_op jit(solution)/shard_map/ppermute | solution.py:32
  227.8 19.0 %copy-start.22 = (bf16[256,1536]{1,0:T(8,128)(2,1)}, bf16[256,1536]{1,0:T(8,128)(2,1)S(1)}, u32[]{:S(2)}) copy-start(bf16[256,1536]{1,0:T(8,128)(2,1)S(1)} %collective-permute-done.1) | copy-start | bytes 2359300
  227.8 33.9 %collective-permute-start.2 = (bf16[256,1536]{1,0:T(8,128)(2,1)S(1)}, bf16[256,1536]{1,0:T(8,128)(2,1)}, u32[]{:S(2)}, u32[]{:S(2)}) collective-permute-start(bf16[256,1536]{1,0:T(8,128)(2,1)S(1)} %collective-permute-done.1), channel_id=1, source_target_pairs={{0,4},{4,8},{8,12},{12,16},{16,20},{20,24},{24,28},{28,0},{1,5},{5... | collective-permute-start | bytes 2359304 | tf_op jit(solution)/shard_map/ppermute | solution.py:30
  243.8 60.3 %collective-permute-start.5 = (bf16[256,1536]{1,0:T(8,128)(2,1)}, bf16[256,1536]{1,0:T(8,128)(2,1)}, u32[]{:S(2)}, u32[]{:S(2)}) collective-permute-start(bf16[256,1536]{1,0:T(8,128)(2,1)} %collective-permute-done.4), channel_id=1, source_target_pairs={{4,0},{8,4},{12,8},{16,12},{20,16},{24,20},{28,24},{0,28},{5,1},{9... | collective-permute-start | bytes 2359304 | tf_op jit(solution)/shard_map/ppermute | solution.py:32
  261.7 43.7 %collective-permute-start.3 = (bf16[256,1536]{1,0:T(8,128)(2,1)}, bf16[256,1536]{1,0:T(8,128)(2,1)}, u32[]{:S(2)}, u32[]{:S(2)}) collective-permute-start(bf16[256,1536]{1,0:T(8,128)(2,1)} %collective-permute-done.2), channel_id=1, source_target_pairs={{0,4},{4,8},{8,12},{12,16},{16,20},{20,24},{24,28},{28,0},{1,5},{5... | collective-permute-start | bytes 2359304 | tf_op jit(solution)/shard_map/ppermute | solution.py:30
  304.1 55.8 %collective-permute-start.6 = (bf16[256,1536]{1,0:T(8,128)(2,1)}, bf16[256,1536]{1,0:T(8,128)(2,1)S(1)}, u32[]{:S(2)}, u32[]{:S(2)}) collective-permute-start(bf16[256,1536]{1,0:T(8,128)(2,1)} %collective-permute-done.5), channel_id=1, source_target_pairs={{4,0},{8,4},{12,8},{16,12},{20,16},{24,20},{28,24},{0,28},{5,1},{9... | collective-permute-start | bytes 2359304 | tf_op jit(solution)/shard_map/ppermute | solution.py:32
  434.9 15.0 %slice-start.6 = ((s8[6291456]{0:T(1024)(128)(4,1)}), s8[4194304]{0:T(1024)(128)(4,1)S(1)}, s32[]{:S(2)}) async-start(s8[6291456]{0:T(1024)(128)(4,1)} %bitcast.269), calls=%async_computation.35 | async-start | bytes 8388608
  434.9 18.4 %slice-start.4 = ((s8[6291456]{0:T(1024)(128)(4,1)}), s8[4194304]{0:T(1024)(128)(4,1)S(1)}, s32[]{:S(2)}) async-start(s8[6291456]{0:T(1024)(128)(4,1)} %bitcast.239), calls=%async_computation.33 | async-start | bytes 8388608
  441.4 12.0 slice-start.5
  441.4 17.1 %slice-start.8 = ((s8[6291456]{0:T(1024)(128)(4,1)}), s8[4194304]{0:T(1024)(128)(4,1)S(1)}, s32[]{:S(2)}) async-start(s8[6291456]{0:T(1024)(128)(4,1)} %bitcast.271), calls=%async_computation.37 | async-start | bytes 8388608
  463.4 255.6 %reduce-scatter.10.cloned.1.call-start = ((), (), s32[]{:S(2)}) async-start(), calls=%async_computation.18 | async-start | bytes 2621440 | tf_op jit(solution)/shard_map/reduce_scatter | solution.py:260
  633.8 15.3 %slice-start = ((s8[16777216]{0:T(1024)(128)(4,1)}), s8[4194304]{0:T(1024)(128)(4,1)S(1)}, s32[]{:S(2)}) async-start(s8[16777216]{0:T(1024)(128)(4,1)} %bitcast.235), calls=%async_computation.29 | async-start | bytes 8388608
  658.9 11.6 copy-start.16
  674.5 89.5 %reduce-scatter.12.cloned.1.call-start = ((), (), s32[]{:S(2)}) async-start(), calls=%async_computation.19 | async-start | bytes 2621440 | tf_op jit(solution)/shard_map/reduce_scatter | solution.py:266
  684.6 130.0 %reduce-scatter.14.cloned.1.call-start = ((), (), s32[]{:S(2)}) async-start(), calls=%async_computation.21 | async-start | bytes 2359296 | tf_op jit(solution)/shard_map/reduce_scatter | solution.py:317
  694.1 171.0 %reduce-scatter.20.cloned.1.call-start = ((), (), s32[]{:S(2)}) async-start(), calls=%async_computation.24 | async-start | bytes 2359296 | tf_op jit(solution)/shard_map/reduce_scatter | solution.py:326
  699.0 295.2 %reduce-scatter.22.cloned.1.call-start = ((), (), s32[]{:S(2)}) async-start(), calls=%async_computation.25 | async-start | bytes 7077888 | tf_op jit(solution)/shard_map/reduce_scatter | solution.py:329
  707.3 417.5 %reduce-scatter.24.cloned.1.call-start = ((), (), s32[]{:S(2)}) async-start(), calls=%async_computation.26 | async-start | bytes 7077888 | tf_op jit(solution)/shard_map/reduce_scatter | solution.py:332
  715.5 482.3 %all-reduce.16.cloned.1.call-start = ((), (), s32[]{:S(2)}) async-start(), calls=%async_computation.20 | async-start | bytes 4194304 | tf_op jit(solution)/shard_map/psum | solution.py:297
  771.0 558.1 %reduce-scatter.26.cloned.1.call-start = ((), (), s32[]{:S(2)}) async-start(), calls=%async_computation.27 | async-start | bytes 7077888 | tf_op jit(solution)/shard_map/reduce_scatter | solution.py:335
  779.3 588.5 %reduce-scatter.16.cloned.1.call-start = ((), (), s32[]{:S(2)}) async-start(), calls=%async_computation.22 | async-start | bytes 1179648 | tf_op jit(solution)/shard_map/reduce_scatter | solution.py:320
  781.4 623.7 %reduce-scatter.18.cloned.1.call-start = ((), (), s32[]{:S(2)}) async-start(), calls=%async_computation.23 | async-start | bytes 1179648 | tf_op jit(solution)/shard_map/reduce_scatter | solution.py:323
  (38 other events, 178.9 us)
Sparse Core Ops, SparseCore 0:
  9.6 24.9 all-gather.10
  36.2 22.2 all-gather.14
  60.6 27.1 all-gather.12
  89.3 28.5 all-gather.18
  119.9 27.3 all-gather.16
  148.7 29.9 all-gather.20
  183.8 102.6 all-reduce.13
  288.0 81.1 all-gather.22
  370.9 63.9 all-gather.24
  463.5 170.2 all-reduce.17
  674.6 44.3 reduce-scatter.9
  721.1 42.8 reduce-scatter.11
  766.3 48.2 reduce-scatter.13
  816.7 48.2 reduce-scatter.19
  867.2 126.9 reduce-scatter.21
  996.4 128.3 reduce-scatter.23
  1127.7 70.0 all-reduce.15
  1200.0 129.0 reduce-scatter.25
  1331.4 36.4 reduce-scatter.15
  1370.0 35.0 reduce-scatter.17
